TPU v7x, 256 devices: a whole 4x4x8 slice. The times are simulated.
256 devices in a mesh: px: 32 (over z, x), py: 8 (over y, core).
Axes of the slice: x: 4, y: 4, z: 8, core: 2. Of those that a mesh axis runs over, the one named last changes fastest.
Arguments:
- field: float32 [512, 512, 1024], P('px', 'py'), may hold values from -120 to 120
- seeds_first: int32 [512, 128], replicated, may hold values from -64 to 63
- seeds_second: int32 [512, 128], replicated, may hold values from -64 to 63
Outputs:
- basis_first: float32 [512, 128], replicated
- basis_second: float32 [512, 128], replicated
- core_tensor: float32 [128, 128, 1024], P('px', 'py')
All inputs are finite; a program needn't handle non-finite values.
Results may differ from a plain program's by a relative error of at most 0.0003.
Values sent between devices are 32-bit elements; how exact they have to be, the bound alone decides.
No kernel may reach another device: no remote copies, remote signals or barrier semaphores. Data moves between devices by JAX's collectives and lax.ppermute only.
A program may use at most 128 MiB of HBM per device.

v0:
```python
import jax
import jax.numpy as jnp
from jax import lax
from jax.sharding import PartitionSpec as P

ITERS = 4


def orthonormal(matrix):
    inner = jnp.dot(matrix.T, matrix, precision=lax.Precision.HIGHEST)
    factor = jnp.linalg.cholesky(inner)
    return jax.scipy.linalg.solve_triangular(factor, matrix.T, lower=True).T


def leading_basis(partial_gram, seeds):
    basis = orthonormal(seeds.astype(jnp.float32))
    gram = lax.psum(partial_gram, ("px", "py"))
    for sweep in range(ITERS):
        basis = orthonormal(jnp.dot(gram, basis, precision=lax.Precision.HIGHEST))
    return basis


def local(field, seeds_first, seeds_second):
    fibers = lax.all_to_all(field, "px", split_axis=1, concat_axis=0, tiled=True)
    whole_first = fibers.shape[0]
    flattened = fibers.reshape(whole_first, -1)
    partial_first = jnp.dot(flattened, flattened.T, precision=lax.Precision.HIGHEST)
    basis_first = leading_basis(partial_first, seeds_first)
    rank_size = basis_first.shape[1]
    reduced = jnp.dot(basis_first.T, flattened, precision=lax.Precision.HIGHEST)
    reduced = reduced.reshape(rank_size, fibers.shape[1], fibers.shape[2])
    slab_fibers = lax.all_to_all(
        lax.all_to_all(reduced, "px", split_axis=0, concat_axis=1, tiled=True),
        "py",
        split_axis=2,
        concat_axis=1,
        tiled=True,
    )
    whole_second = slab_fibers.shape[1]
    turned = jnp.transpose(slab_fibers, (1, 0, 2)).reshape(whole_second, -1)
    partial_second = jnp.dot(turned, turned.T, precision=lax.Precision.HIGHEST)
    basis_second = leading_basis(partial_second, seeds_second)
    core_tensor = jnp.einsum(
        "jb,ajp->abp", basis_second, slab_fibers, precision=lax.Precision.HIGHEST
    )
    core_tensor = lax.all_to_all(core_tensor, "py", split_axis=1, concat_axis=2, tiled=True)
    return (basis_first, basis_second, core_tensor)


def solution(mesh):
    placed = (P("px", "py", None), P(), P())
    return jax.shard_map(
        local,
        mesh=mesh,
        in_specs=placed,
        out_specs=(P(), P(), P("px", "py", None)),
        check_vma=False,
    )
```

profile of v0, /device:TPU:1, one launch (start us, length us, event | category | flops | bytes accessed | tf_op | source)
XLA Modules:
  0.0 948.8 jit_solution(8441352326940024443)
XLA Ops:
  13.8 12.1 %all-to-all-start = ((f32[16,64,1024]{2,0,1:T(8,128)}), f32[16,64,1024]{2,0,1:T(8,128)}, u32[]{:S(2)}, u32[]{:S(2)}) async-start(f32[16,64,1024]{2,0,1:T(8,128)} %copy.84), calls=%async_computation | async-start | bytes 8388608 | tf_op jit(solution)/shard_map/all_to_all | solution.py:24
  27.0 11.7 %cholesky.164 = f32[128,128]{1,0:T(8,128)S(1)} custom-call(f32[128,128]{1,0:T(8,128)S(1)} %fusion.58), custom_call_target="Cholesky" | custom-call | tf_op jit(solution)/shard_map/jit(cholesky)/cholesky | solution.py:11
  38.7 80.2 %all-to-all-done = f32[16,64,1024]{2,0,1:T(8,128)} async-done(((f32[16,64,1024]{2,0,1:T(8,128)}), f32[16,64,1024]{2,0,1:T(8,128)}, u32[]{:S(2)}, u32[]{:S(2)}) %all-to-all-start) | async-done | bytes 4194336 | tf_op jit(solution)/shard_map/all_to_all | solution.py:24
  138.1 9.8 %custom-call.14 = f32[1,128,128]{1,2,0:T(8,128)S(1)} custom-call(f32[1,128,128]{2,1,0:T(8,128)S(1)} %fusion.29), custom_call_target="InvertDiagBlocksLowerTriangular" | custom-call | tf_op jit(solution)/shard_map/jit(_solve_triangular)/triangular_solve | solution.py:12
  153.9 237.6 %all-reduce.3.cloned.1.call-done = f32[512,512]{1,0:T(8,128)} async-done(((f32[512,512]{1,0:T(8,128)}), f32[512,512]{1,0:T(8,128)}) %all-reduce.3.cloned.1.call-update) | async-done | bytes 1048592 | tf_op jit(solution)/shard_map/psum | solution.py:17
  394.5 11.7 %cholesky.175 = f32[128,128]{1,0:T(8,128)S(1)} custom-call(f32[128,128]{1,0:T(8,128)S(1)} %fusion.56), custom_call_target="Cholesky" | custom-call | tf_op jit(solution)/shard_map/jit(cholesky)/cholesky | solution.py:11
  407.6 9.8 %custom-call.15 = f32[1,128,128]{1,2,0:T(8,128)S(1)} custom-call(f32[1,128,128]{2,1,0:T(8,128)S(1)} %fusion.30), custom_call_target="InvertDiagBlocksLowerTriangular" | custom-call | tf_op jit(solution)/shard_map/jit(_solve_triangular)/triangular_solve | solution.py:12
  420.8 11.9 %cholesky.186 = f32[128,128]{1,0:T(8,128)S(1)} custom-call(f32[128,128]{1,0:T(8,128)S(1)} %fusion.54), custom_call_target="Cholesky" | custom-call | tf_op jit(solution)/shard_map/jit(cholesky)/cholesky | solution.py:11
  434.0 9.8 %custom-call.16 = f32[1,128,128]{1,2,0:T(8,128)S(1)} custom-call(f32[1,128,128]{2,1,0:T(8,128)S(1)} %fusion.31), custom_call_target="InvertDiagBlocksLowerTriangular" | custom-call | tf_op jit(solution)/shard_map/jit(_solve_triangular)/triangular_solve | solution.py:12
  446.0 11.7 %cholesky.197 = f32[128,128]{1,0:T(8,128)S(1)} custom-call(f32[128,128]{1,0:T(8,128)S(1)} %fusion.52), custom_call_target="Cholesky" | custom-call | tf_op jit(solution)/shard_map/jit(cholesky)/cholesky | solution.py:11
  459.0 9.8 %custom-call.17 = f32[1,128,128]{1,2,0:T(8,128)S(1)} custom-call(f32[1,128,128]{2,1,0:T(8,128)S(1)} %fusion.32), custom_call_target="InvertDiagBlocksLowerTriangular" | custom-call | tf_op jit(solution)/shard_map/jit(_solve_triangular)/triangular_solve | solution.py:12
  471.3 11.7 %cholesky.208 = f32[128,128]{1,0:T(8,128)S(1)} custom-call(f32[128,128]{1,0:T(8,128)S(1)} %fusion.50), custom_call_target="Cholesky" | custom-call | tf_op jit(solution)/shard_map/jit(cholesky)/cholesky | solution.py:11
  484.4 9.8 %custom-call.18 = f32[1,128,128]{1,2,0:T(8,128)S(1)} custom-call(f32[1,128,128]{2,1,0:T(8,128)S(1)} %fusion.33), custom_call_target="InvertDiagBlocksLowerTriangular" | custom-call | tf_op jit(solution)/shard_map/jit(_solve_triangular)/triangular_solve | solution.py:12
  502.1 35.5 %all_to_all.69 = f32[128,2,1024]{2,1,0:T(2,128)S(1)} all-to-all(f32[128,2,1024]{2,1,0:T(2,128)S(1)} %copy.92), channel_id=1, replica_groups=mesh['px'=32,'py'=8] {'px'}, dimensions={0} | all-to-all | bytes 2097152 | tf_op jit(solution)/shard_map/all_to_all | solution.py:33
  548.8 11.7 %cholesky.219 = f32[128,128]{1,0:T(8,128)S(1)} custom-call(f32[128,128]{1,0:T(8,128)S(1)} %fusion.48), custom_call_target="Cholesky" | custom-call | tf_op jit(solution)/shard_map/jit(cholesky)/cholesky | solution.py:11
  573.5 9.8 %custom-call.19 = f32[1,128,128]{1,2,0:T(8,128)S(1)} custom-call(f32[1,128,128]{2,1,0:T(8,128)S(1)} %fusion.34), custom_call_target="InvertDiagBlocksLowerTriangular" | custom-call | tf_op jit(solution)/shard_map/jit(_solve_triangular)/triangular_solve | solution.py:12
  583.8 238.5 %all-reduce.5.cloned.1.call-done = f32[512,512]{1,0:T(8,128)} async-done(((f32[512,512]{1,0:T(8,128)}), f32[512,512]{1,0:T(8,128)}) %all-reduce.5.cloned.1.call-update) | async-done | bytes 1048592 | tf_op jit(solution)/shard_map/psum | solution.py:17
  825.2 11.7 %cholesky.230 = f32[128,128]{1,0:T(8,128)S(1)} custom-call(f32[128,128]{1,0:T(8,128)S(1)} %fusion.46), custom_call_target="Cholesky" | custom-call | tf_op jit(solution)/shard_map/jit(cholesky)/cholesky | solution.py:11
  838.3 10.2 %custom-call.20 = f32[1,128,128]{1,2,0:T(8,128)S(1)} custom-call(f32[1,128,128]{2,1,0:T(8,128)S(1)} %fusion.35), custom_call_target="InvertDiagBlocksLowerTriangular" | custom-call | tf_op jit(solution)/shard_map/jit(_solve_triangular)/triangular_solve | solution.py:12
  851.8 11.7 %cholesky.241 = f32[128,128]{1,0:T(8,128)S(1)} custom-call(f32[128,128]{1,0:T(8,128)S(1)} %fusion.44), custom_call_target="Cholesky" | custom-call | tf_op jit(solution)/shard_map/jit(cholesky)/cholesky | solution.py:11
  864.9 9.8 %custom-call.21 = f32[1,128,128]{1,2,0:T(8,128)S(1)} custom-call(f32[1,128,128]{2,1,0:T(8,128)S(1)} %fusion.36), custom_call_target="InvertDiagBlocksLowerTriangular" | custom-call | tf_op jit(solution)/shard_map/jit(_solve_triangular)/triangular_solve | solution.py:12
  876.8 11.9 %cholesky.252 = f32[128,128]{1,0:T(8,128)S(1)} custom-call(f32[128,128]{1,0:T(8,128)S(1)} %fusion.42), custom_call_target="Cholesky" | custom-call | tf_op jit(solution)/shard_map/jit(cholesky)/cholesky | solution.py:11
  902.0 11.7 %cholesky.263 = f32[128,128]{1,0:T(8,128)S(1)} custom-call(f32[128,128]{1,0:T(8,128)S(1)} %fusion.40), custom_call_target="Cholesky" | custom-call | tf_op jit(solution)/shard_map/jit(cholesky)/cholesky | solution.py:11
  915.0 10.0 %custom-call.23 = f32[1,128,128]{1,2,0:T(8,128)S(1)} custom-call(f32[1,128,128]{2,1,0:T(8,128)S(1)} %fusion.38), custom_call_target="InvertDiagBlocksLowerTriangular" | custom-call | tf_op jit(solution)/shard_map/jit(_solve_triangular)/triangular_solve | solution.py:12
  (120 shorter events, 123.6 us)
Async XLA Ops:
  13.8 12.5 %copy-start.3 = (s32[512,128]{1,0:T(8,128)S(1)}, s32[512,128]{1,0:T(8,128)}, u32[]{:S(2)}) copy-start(s32[512,128]{1,0:T(8,128)} %param.7) | copy-start | bytes 786436
  13.8 105.2 %all-to-all-start = ((f32[16,64,1024]{2,0,1:T(8,128)}), f32[16,64,1024]{2,0,1:T(8,128)}, u32[]{:S(2)}, u32[]{:S(2)}) async-start(f32[16,64,1024]{2,0,1:T(8,128)} %copy.84), calls=%async_computation | async-start | bytes 8388608 | tf_op jit(solution)/shard_map/all_to_all | solution.py:24
  25.9 365.6 %all-reduce.3.cloned.1.call-start = ((), (), s32[]{:S(2)}) async-start(), calls=%async_computation.4 | async-start | bytes 2097152 | tf_op jit(solution)/shard_map/psum | solution.py:17
  126.4 1.9 copy-start
  391.5 52.7 %copy-start.1 = (f32[512,512]{1,0:T(8,128)S(1)}, f32[512,512]{1,0:T(8,128)}, u32[]{:S(2)}) copy-start(f32[512,512]{1,0:T(8,128)} %all-reduce.3.cloned.1.call-done) | copy-start | bytes 3145732
  539.0 9.0 copy-start.4
  541.8 21.3 %all-to-all-start.2 = ((f32[8,1,32768]{2,1,0:T(1,128)}), f32[8,1,32768]{2,1,0:T(1,128)S(1)}, u32[]{:S(2)}, u32[]{:S(2)}) async-start(f32[8,1,32768]{2,1,0:T(1,128)} %reshape.25), calls=%async_computation.2 | async-start | bytes 2097152 | tf_op jit(solution)/shard_map/all_to_all | solution.py:32
  548.1 274.2 %all-reduce.5.cloned.1.call-start = ((), (), s32[]{:S(2)}) async-start(), calls=%async_computation.5 | async-start | bytes 2097152 | tf_op jit(solution)/shard_map/psum | solution.py:17
  569.3 14.1 %copy-start.5 = (s32[512,128]{1,0:T(8,128)S(1)}, s32[512,128]{1,0:T(8,128)}, u32[]{:S(2)}) copy-start(s32[512,128]{1,0:T(8,128)} %param.8) | copy-start | bytes 786436
  822.2 52.9 %copy-start.2 = (f32[512,512]{1,0:T(8,128)S(1)}, f32[512,512]{1,0:T(8,128)}, u32[]{:S(2)}) copy-start(f32[512,512]{1,0:T(8,128)} %all-reduce.5.cloned.1.call-done) | copy-start | bytes 3145732
  928.1 12.9 %all-to-all-start.3 = ((f32[4,128,128]{2,0,1:T(4,128)}), f32[4,128,128]{2,0,1:T(4,128)S(1)}, u32[]{:S(2)}, u32[]{:S(2)}) async-start(f32[4,128,128]{2,0,1:T(4,128)} %copy.103), calls=%async_computation.3 | async-start | bytes 524288 | tf_op jit(solution)/shard_map/all_to_all | solution.py:46
Sparse Core Ops, SparseCore 0:
  136.9 254.5 all-reduce.2
  572.3 249.8 all-reduce.4
where the time goes:
time: 952 us; the launch traced here: 949 us
  waiting for transfers between devices  564 us (59%)
  other arithmetic  233 us (24%)
  matrix products  43 us (5%)
  blocking collectives  35.5 us (4%)
  local copies, waits for them, and re-layouts  33.7 us (4%)
  starting transfers between devices  25.1 us (3%)
  between operations  14.9 us (2%)
    psum x2, waiting for transfers between devices, leading_basis(): gram = lax.psum(partial_gram, ('px', 'py'))  476 us
    another operation x30, other arithmetic, orthonormal(): factor = jnp.linalg.cholesky(inner)  124 us
    another operation x20, other arithmetic, orthonormal(): return jax.scipy.linalg.solve_triangular(factor, matrix.T, lower=True).T  105 us
    all_to_all x1, waiting for transfers between devices, local(): lax.all_to_all(field, 'px', split_axis=1, concat_axis=0, tiled=True)  80.2 us
    all_to_all x1, blocking collectives, local(): lax.all_to_all(reduced, 'px', split_axis=0, concat_axis=1, tiled=True)  35.5 us
  transfers between devices with their start and end apart: 5, of which 5 were waited for; matrix products, arithmetic and copies ran while one was open for 6% of the time, Pallas kernels for 0%

commit v1 on v0

--- a/solution.py
+++ b/solution.py
@@ -14,7 +14,7 @@
 
 def leading_basis(partial_gram, seeds):
     basis = orthonormal(seeds.astype(jnp.float32))
-    gram = lax.psum(partial_gram, ("px", "py"))
+    gram = lax.psum(lax.psum(partial_gram, "py"), "px")
     for sweep in range(ITERS):
         basis = orthonormal(jnp.dot(gram, basis, precision=lax.Precision.HIGHEST))
     return basis

time: 952 us -> 868 us (0.912)
  waiting for transfers between devices: 564 us -> 376 us
  blocking collectives: 35.5 us -> 159 us
  starting transfers between devices: 25.1 us -> 9.93 us
    all_to_all x0 -> x2, blocking collectives: none -> 132 us  [the longest x1 105 us: local(): lax.all_to_all(field, 'px', split_axis=1, concat_axis=0, tiled=True)]
    psum x2 -> x4, waiting for transfers between devices: 476 us -> 371 us  [leading_basis(): gram = lax.psum(lax.psum(partial_gram, 'py'), 'px')]
    all_to_all x2 -> x0, waiting for transfers between devices: 82.9 us -> none  [the longest x1 80.2 us: local(): lax.all_to_all(field, 'px', split_axis=1, concat_axis=0, tiled=True)]
    all_to_all x2 -> x0, starting transfers between devices: 18.4 us -> none  [the longest x1 12.1 us: local(): lax.all_to_all(field, 'px', split_axis=1, concat_axis=0, tiled=True)]
where the time goes in v1:
time: 868 us; the launch traced here: 865 us
  waiting for transfers between devices  376 us (43%)
  other arithmetic  233 us (27%)
  blocking collectives  159 us (18%)
  matrix products  43.1 us (5%)
  local copies, waits for them, and re-layouts  28.6 us (3%)
  between operations  14.8 us (2%)
  starting transfers between devices  9.93 us (1%)
    psum x4, waiting for transfers between devices, leading_basis(): gram = lax.psum(lax.psum(partial_gram, 'py'), 'px')  371 us
    another operation x30, other arithmetic, orthonormal(): factor = jnp.linalg.cholesky(inner)  125 us
    all_to_all x1, blocking collectives, local(): lax.all_to_all(field, 'px', split_axis=1, concat_axis=0, tiled=True)  105 us
    another operation x20, other arithmetic, orthonormal(): return jax.scipy.linalg.solve_triangular(factor, matrix.T, lower=True).T  105 us
    all_to_all x1, blocking collectives, local(): lax.all_to_all(reduced, 'px', split_axis=0, concat_axis=1, tiled=True)  27.5 us
    all_to_all x1, blocking collectives, local(): lax.all_to_all(lax.all_to_all(reduced, 'px', split_axis=0, concat_axis=1,...  26.4 us
  transfers between devices with their start and end apart: 5, of which 5 were waited for; matrix products, arithmetic and copies ran while one was open for 6% of the time, Pallas kernels for 0%

profile of v1, /device:TPU:1, one launch (start us, length us, event | category | flops | bytes accessed | tf_op | source)
XLA Modules:
  0.0 864.5 jit_solution(4628999459914114798)
XLA Ops:
  11.8 105.3 %all_to_all.69 = f32[16,64,1024]{2,0,1:T(8,128)S(1)} all-to-all(f32[16,64,1024]{2,0,1:T(8,128)S(1)} %copy.84), channel_id=1, replica_groups=mesh['px'=32,'py'=8] {'px'}, dimensions={1} | all-to-all | bytes 8388608 | tf_op jit(solution)/shard_map/all_to_all | solution.py:24
  132.9 65.0 %all-reduce.5.cloned.1.call-done = f32[512,512]{1,0:T(8,128)} async-done(((f32[512,512]{1,0:T(8,128)}), f32[512,512]{1,0:T(8,128)}) %all-reduce.5.cloned.1.call-update) | async-done | bytes 1048592 | tf_op jit(solution)/shard_map/psum | solution.py:17
  198.7 11.7 %cholesky.164 = f32[128,128]{1,0:T(8,128)S(1)} custom-call(f32[128,128]{1,0:T(8,128)S(1)} %fusion.58), custom_call_target="Cholesky" | custom-call | tf_op jit(solution)/shard_map/jit(cholesky)/cholesky | solution.py:11
  211.8 9.8 %custom-call.14 = f32[1,128,128]{1,2,0:T(8,128)S(1)} custom-call(f32[1,128,128]{2,1,0:T(8,128)S(1)} %fusion.29), custom_call_target="InvertDiagBlocksLowerTriangular" | custom-call | tf_op jit(solution)/shard_map/jit(_solve_triangular)/triangular_solve | solution.py:12
  227.6 120.0 %all-reduce.7.cloned.1.call-done = f32[512,512]{1,0:T(8,128)} async-done(((f32[512,512]{1,0:T(8,128)}), f32[512,512]{1,0:T(8,128)}) %all-reduce.7.cloned.1.call-update) | async-done | bytes 1048592 | tf_op jit(solution)/shard_map/psum | solution.py:17
  350.6 11.7 %cholesky.175 = f32[128,128]{1,0:T(8,128)S(1)} custom-call(f32[128,128]{1,0:T(8,128)S(1)} %fusion.56), custom_call_target="Cholesky" | custom-call | tf_op jit(solution)/shard_map/jit(cholesky)/cholesky | solution.py:11
  363.7 9.8 %custom-call.15 = f32[1,128,128]{1,2,0:T(8,128)S(1)} custom-call(f32[1,128,128]{2,1,0:T(8,128)S(1)} %fusion.30), custom_call_target="InvertDiagBlocksLowerTriangular" | custom-call | tf_op jit(solution)/shard_map/jit(_solve_triangular)/triangular_solve | solution.py:12
  376.8 11.9 %cholesky.186 = f32[128,128]{1,0:T(8,128)S(1)} custom-call(f32[128,128]{1,0:T(8,128)S(1)} %fusion.54), custom_call_target="Cholesky" | custom-call | tf_op jit(solution)/shard_map/jit(cholesky)/cholesky | solution.py:11
  390.1 9.8 %custom-call.16 = f32[1,128,128]{1,2,0:T(8,128)S(1)} custom-call(f32[1,128,128]{2,1,0:T(8,128)S(1)} %fusion.31), custom_call_target="InvertDiagBlocksLowerTriangular" | custom-call | tf_op jit(solution)/shard_map/jit(_solve_triangular)/triangular_solve | solution.py:12
  402.0 11.7 %cholesky.197 = f32[128,128]{1,0:T(8,128)S(1)} custom-call(f32[128,128]{1,0:T(8,128)S(1)} %fusion.52), custom_call_target="Cholesky" | custom-call | tf_op jit(solution)/shard_map/jit(cholesky)/cholesky | solution.py:11
  415.1 9.8 %custom-call.17 = f32[1,128,128]{1,2,0:T(8,128)S(1)} custom-call(f32[1,128,128]{2,1,0:T(8,128)S(1)} %fusion.32), custom_call_target="InvertDiagBlocksLowerTriangular" | custom-call | tf_op jit(solution)/shard_map/jit(_solve_triangular)/triangular_solve | solution.py:12
  427.4 11.7 %cholesky.208 = f32[128,128]{1,0:T(8,128)S(1)} custom-call(f32[128,128]{1,0:T(8,128)S(1)} %fusion.50), custom_call_target="Cholesky" | custom-call | tf_op jit(solution)/shard_map/jit(cholesky)/cholesky | solution.py:11
  440.5 9.8 %custom-call.18 = f32[1,128,128]{1,2,0:T(8,128)S(1)} custom-call(f32[1,128,128]{2,1,0:T(8,128)S(1)} %fusion.33), custom_call_target="InvertDiagBlocksLowerTriangular" | custom-call | tf_op jit(solution)/shard_map/jit(_solve_triangular)/triangular_solve | solution.py:12
  458.2 27.5 %all_to_all.70 = f32[128,2,1024]{2,1,0:T(2,128)S(1)} all-to-all(f32[128,2,1024]{2,1,0:T(2,128)S(1)} %copy.92), channel_id=1, replica_groups=mesh['px'=32,'py'=8] {'px'}, dimensions={0} | all-to-all | bytes 2097152 | tf_op jit(solution)/shard_map/all_to_all | solution.py:33
  489.1 26.4 %all_to_all.71 = f32[8,1,32768]{2,1,0:T(1,128)S(1)} all-to-all(f32[8,1,32768]{2,1,0:T(1,128)S(1)} %reshape.25), channel_id=1, replica_groups=mesh['px'=32,'py'=8] {'py'}, dimensions={0} | all-to-all | bytes 2097152 | tf_op jit(solution)/shard_map/all_to_all | solution.py:32
  524.6 61.0 %all-reduce.9.cloned.1.call-done = f32[512,512]{1,0:T(8,128)} async-done(((f32[512,512]{1,0:T(8,128)}), f32[512,512]{1,0:T(8,128)}) %all-reduce.9.cloned.1.call-update) | async-done | bytes 1048592 | tf_op jit(solution)/shard_map/psum | solution.py:17
  586.3 11.7 %cholesky.219 = f32[128,128]{1,0:T(8,128)S(1)} custom-call(f32[128,128]{1,0:T(8,128)S(1)} %fusion.48), custom_call_target="Cholesky" | custom-call | tf_op jit(solution)/shard_map/jit(cholesky)/cholesky | solution.py:11
  599.4 9.8 %custom-call.19 = f32[1,128,128]{1,2,0:T(8,128)S(1)} custom-call(f32[1,128,128]{2,1,0:T(8,128)S(1)} %fusion.34), custom_call_target="InvertDiagBlocksLowerTriangular" | custom-call | tf_op jit(solution)/shard_map/jit(_solve_triangular)/triangular_solve | solution.py:12
  609.6 125.4 %all-reduce.11.cloned.1.call-done = f32[512,512]{1,0:T(8,128)} async-done(((f32[512,512]{1,0:T(8,128)}), f32[512,512]{1,0:T(8,128)}) %all-reduce.11.cloned.1.call-update) | async-done | bytes 1048592 | tf_op jit(solution)/shard_map/psum | solution.py:17
  738.0 12.1 %cholesky.230 = f32[128,128]{1,0:T(8,128)S(1)} custom-call(f32[128,128]{1,0:T(8,128)S(1)} %fusion.46), custom_call_target="Cholesky" | custom-call | tf_op jit(solution)/shard_map/jit(cholesky)/cholesky | solution.py:11
  751.5 9.8 %custom-call.20 = f32[1,128,128]{1,2,0:T(8,128)S(1)} custom-call(f32[1,128,128]{2,1,0:T(8,128)S(1)} %fusion.35), custom_call_target="InvertDiagBlocksLowerTriangular" | custom-call | tf_op jit(solution)/shard_map/jit(_solve_triangular)/triangular_solve | solution.py:12
  764.6 11.7 %cholesky.241 = f32[128,128]{1,0:T(8,128)S(1)} custom-call(f32[128,128]{1,0:T(8,128)S(1)} %fusion.44), custom_call_target="Cholesky" | custom-call | tf_op jit(solution)/shard_map/jit(cholesky)/cholesky | solution.py:11
  789.8 11.7 %cholesky.252 = f32[128,128]{1,0:T(8,128)S(1)} custom-call(f32[128,128]{1,0:T(8,128)S(1)} %fusion.42), custom_call_target="Cholesky" | custom-call | tf_op jit(solution)/shard_map/jit(cholesky)/cholesky | solution.py:11
  814.8 11.9 %cholesky.263 = f32[128,128]{1,0:T(8,128)S(1)} custom-call(f32[128,128]{1,0:T(8,128)S(1)} %fusion.40), custom_call_target="Cholesky" | custom-call | tf_op jit(solution)/shard_map/jit(cholesky)/cholesky | solution.py:11
  (122 shorter events, 132.5 us)
Async XLA Ops:
  7.2 190.8 %all-reduce.5.cloned.1.call-start = ((), (), s32[]{:S(2)}) async-start(), calls=%async_computation.4 | async-start | bytes 2097152 | tf_op jit(solution)/shard_map/psum | solution.py:17
  122.5 1.9 copy-start
  124.4 73.6 %copy-start.3 = (s32[512,128]{1,0:T(8,128)S(1)}, s32[512,128]{1,0:T(8,128)}, u32[]{:S(2)}) copy-start(s32[512,128]{1,0:T(8,128)} %param.7) | copy-start | bytes 786436
  132.8 214.8 %all-reduce.7.cloned.1.call-start = ((), (), s32[]{:S(2)}) async-start(), calls=%async_computation.5 | async-start | bytes 2097152 | tf_op jit(solution)/shard_map/psum | solution.py:17
  198.0 387.6 %all-reduce.9.cloned.1.call-start = ((), (), s32[]{:S(2)}) async-start(), calls=%async_computation.6 | async-start | bytes 2097152 | tf_op jit(solution)/shard_map/psum | solution.py:17
  347.6 52.7 %copy-start.1 = (f32[512,512]{1,0:T(8,128)S(1)}, f32[512,512]{1,0:T(8,128)}, u32[]{:S(2)}) copy-start(f32[512,512]{1,0:T(8,128)} %all-reduce.7.cloned.1.call-done) | copy-start | bytes 3145732
  521.4 64.2 %copy-start.4 = (s32[512,128]{1,0:T(8,128)S(1)}, s32[512,128]{1,0:T(8,128)}, u32[]{:S(2)}) copy-start(s32[512,128]{1,0:T(8,128)} %param.8) | copy-start | bytes 786436
  524.3 210.7 %all-reduce.11.cloned.1.call-start = ((), (), s32[]{:S(2)}) async-start(), calls=%async_computation.7 | async-start | bytes 2097152 | tf_op jit(solution)/shard_map/psum | solution.py:17
  735.0 52.9 %copy-start.2 = (f32[512,512]{1,0:T(8,128)S(1)}, f32[512,512]{1,0:T(8,128)}, u32[]{:S(2)}) copy-start(f32[512,512]{1,0:T(8,128)} %all-reduce.11.cloned.1.call-done) | copy-start | bytes 3145732
  840.9 16.1 %all-to-all-start.3 = ((f32[4,128,128]{2,0,1:T(4,128)}), f32[4,128,128]{2,0,1:T(4,128)S(1)}, u32[]{:S(2)}, u32[]{:S(2)}) async-start(f32[4,128,128]{2,0,1:T(4,128)} %copy.103), calls=%async_computation.3 | async-start | bytes 524288 | tf_op jit(solution)/shard_map/all_to_all | solution.py:46
Sparse Core Ops, SparseCore 0:
  133.0 64.9 all-reduce.4
  201.4 146.1 all-reduce.6
  524.4 61.0 all-reduce.8
  588.8 146.1 all-reduce.10
